TPU v7x, 256 devices: a whole 4x4x8 slice. The times are simulated.
256 devices in a mesh: ctx: 16 (over x_hi, y, core), head: 16 (over x_lo, z).
Axes of the slice: x: 4 (x_hi: 2, x_lo: 2; x = x_hi * 2 + x_lo), y: 4, z: 8, core: 2. Of those that a mesh axis runs over, the one named last changes fastest.
Arguments:
- new_states: bfloat16 [2048, 8192], P('ctx', 'head'), may hold values from -6 to 6
- query_weight: bfloat16 [8192, 8192], P(None, 'head'), may hold values from -0.0625 to 0.0625
- key_weight: bfloat16 [8192, 1024], P(None, 'head'), may hold values from -0.0625 to 0.0625
- value_weight: bfloat16 [8192, 1024], P(None, 'head'), may hold values from -0.0625 to 0.0625
- cache_keys: bfloat16 [18432, 1024], P('ctx', 'head'), may hold values from -480 to 480
- cache_values: bfloat16 [18432, 1024], P('ctx', 'head'), may hold values from -6 to 6
- new_positions: int32 [2048], P('ctx'), may hold values from 18432 to 20479, as said below
Outputs:
- attended: bfloat16 [2048, 8192], P('ctx', 'head')
Inputs may be any that keep to these rules, and one draw needn't show every extreme that they name: `new_positions`: the appended rows hold each position from 18432 to 20479 once, in runs of 8 consecutive positions.
All inputs are finite; a program needn't handle non-finite values.
Results may differ from a plain program's by a relative error of at most 0.04.
Values may be sent and summed in bfloat16 or wider, within the bound.
A program may use at most 128 MiB of HBM per device.

v0:
```python
import math

import jax
import jax.numpy as jnp
from jax import lax
from jax.sharding import PartitionSpec as P

THETA = 500000.0
NEGATIVE = -1e30


def swapped(block, axis, stride):
    count = lax.axis_size(axis)
    route = []
    for low in range(count):
        high = low | 1 << stride
        if high != low and high < count:
            route += [(low, high), (high, low)]
    return lax.ppermute(block, axis, route)


def rotary(values, positions):
    half_width = values.shape[-1] // 2
    freq_index = jnp.arange(half_width, dtype=jnp.float32)
    inverse = jnp.exp(freq_index * (-2.0 * math.log(THETA) / values.shape[-1]))
    angles = positions.astype(jnp.float32)[:, None] * inverse[None, :]
    cosine = jnp.cos(angles)[:, None, :]
    sine_part = jnp.sin(angles)[:, None, :]
    lower_part = values[..., :half_width]
    upper_part = values[..., half_width:]
    return jnp.concatenate(
        [
            lower_part * cosine - upper_part * sine_part,
            upper_part * cosine + lower_part * sine_part,
        ],
        axis=-1,
    )


def tile_scores(query_block, query_positions, keys_here, positions_here):
    scores = jnp.einsum("qhd,kd->hqk", query_block, keys_here, preferred_element_type=jnp.float32)
    visible = positions_here[None, None, :] <= query_positions[None, :, None]
    return (jnp.where(visible, scores, NEGATIVE), visible)


def per_device(
    new_states, query_weight, key_weight, value_weight, cache_keys, cache_values, new_positions
):
    row_count = new_states.shape[0]
    half_width = key_weight.shape[1]
    head_size = 2 * half_width
    query_cols = query_weight.shape[1]
    heads = query_cols // head_size
    cached_rows = cache_keys.shape[0]
    both_weight = jnp.concatenate([key_weight, value_weight], axis=1)
    piece = lax.all_gather(new_states, "head", axis=1, tiled=True)
    query_sum = jnp.dot(piece, query_weight, preferred_element_type=jnp.float32)
    pair_sum = jnp.dot(piece, both_weight, preferred_element_type=jnp.float32)
    queries = (
        rotary(query_sum.reshape(row_count, heads, head_size), new_positions) * head_size ** (-0.5)
    ).astype(jnp.bfloat16)
    new_pair = pair_sum.astype(jnp.bfloat16)
    own_halves = jnp.concatenate(
        [jnp.concatenate([cache_keys, cache_values], axis=1), new_pair], axis=0
    )
    other_halves = swapped(own_halves, "head", 0)
    lower_bit = lax.axis_index("head") % 2 == 0
    lower_pair = jnp.where(lower_bit, own_halves, other_halves)
    upper_pair = jnp.where(lower_bit, other_halves, own_halves)
    keys_full = jnp.concatenate([lower_pair[:, :half_width], upper_pair[:, :half_width]], axis=1)
    values_full = jnp.concatenate([lower_pair[:, half_width:], upper_pair[:, half_width:]], axis=1)
    turned = rotary(keys_full[cached_rows:].astype(jnp.float32)[:, None, :], new_positions)[
        :, 0, :
    ].astype(jnp.bfloat16)
    keys_full = jnp.concatenate([keys_full[:cached_rows], turned], axis=0)
    key_block = jnp.concatenate([keys_full, values_full], axis=1)
    key_positions = jnp.concatenate([jnp.zeros((cached_rows,), jnp.int32), new_positions])
    block_rows = key_block.shape[0]

    def absorb_block(running, block_pair):
        blocks, block_positions = block_pair
        highest, weight_sum, accumulated = running
        scores, visible = tile_scores(
            queries, new_positions, blocks[:, :head_size], block_positions
        )
        new_highest = jnp.maximum(highest, jnp.max(scores, axis=2))
        factor = jnp.exp(highest - new_highest)
        weights = jnp.where(visible, jnp.exp(scores - new_highest[:, :, None]), 0.0)
        weight_sum = weight_sum * factor + jnp.sum(weights, axis=2)
        accumulated = accumulated * factor[:, :, None] + jnp.einsum(
            "hqk,kd->hqd",
            weights.astype(jnp.bfloat16),
            blocks[:, head_size:],
            preferred_element_type=jnp.float32,
        )
        return (new_highest, weight_sum, accumulated)

    def stepper(inner, block_pair):
        return (absorb_block(inner, block_pair), None)

    start_state = (
        jnp.full((heads, row_count), NEGATIVE, jnp.float32),
        jnp.zeros((heads, row_count), jnp.float32),
        jnp.zeros((heads, row_count, head_size), jnp.float32),
    )
    running = start_state
    blocks = lax.all_gather(key_block, "ctx", axis=0, tiled=True)
    block_positions = lax.all_gather(key_positions, "ctx", axis=0, tiled=True)
    piece_rows = blocks.shape[0]
    stacked = (
        blocks.reshape(piece_rows // block_rows, block_rows, 2 * head_size),
        block_positions.reshape(piece_rows // block_rows, block_rows),
    )
    running, _unused = lax.scan(stepper, running, stacked)
    highest, weight_sum, accumulated = running
    attended = (
        (accumulated / weight_sum[:, :, None])
        .transpose(1, 0, 2)
        .reshape(row_count, query_cols)
        .astype(jnp.bfloat16)
    )
    return attended


def solution(mesh):
    placed = (
        P("ctx", "head"),
        P(None, "head"),
        P(None, "head"),
        P(None, "head"),
        P("ctx", "head"),
        P("ctx", "head"),
        P("ctx"),
    )
    return jax.shard_map(
        per_device, mesh=mesh, in_specs=placed, out_specs=P("ctx", "head"), check_vma=False
    )
```

profile of v0, /device:TPU:32, one launch (start us, length us, event | category | flops | bytes accessed | tf_op | source)
XLA Modules:
  0.0 252.1 jit_solution(5024837956362516789)
XLA Ops:
  6.5 0.7 all-gather.4.cloned.1.call-update
  7.3 75.1 %all-gather.4.cloned.1.call-done = bf16[128,8192]{1,0:T(8,128)(2,1)} async-done(((bf16[128,512]{1,0:T(8,128)(2,1)}), bf16[128,8192]{1,0:T(8,128)(2,1)}) %all-gather.4.cloned.1.call-update) | async-done | bytes 2097168 | tf_op jit(solution)/shard_map/all_gather | solution.py:56
  82.5 2.9 %fusion.20 = bf16[128,128]{1,0:T(8,128)(2,1)S(1)} fusion(bf16[128,8192]{1,0:T(8,128)(2,1)} %all-gather.4.cloned.1.call-done, bf16[8192,64]{0,1:T(8,128)(2,1)} %param.12, bf16[8192,64]{0,1:T(8,128)(2,1)} %param.11), kind=kOutput, calls=%fused_computation.26 | convolution fusion | flops 272646144 | bytes 4227072 | tf_op jit(solution)/shard_map/dot_general | solution.py:58
  85.6 1.4 collective-permute-start
  87.0 5.8 %collective-permute-done = bf16[1280,128]{0,1:T(8,128)(2,1)S(1)} collective-permute-done((bf16[1280,128]{0,1:T(8,128)(2,1)S(1)}, bf16[1280,128]{0,1:T(8,128)(2,1)S(1)}, u32[]{:S(2)}, u32[]{:S(2)}) %collective-permute-start) | collective-permute-done | bytes 327712 | tf_op jit(solution)/shard_map/ppermute | solution.py:19
  93.2 0.9 pad_maximum_fusion
  94.2 24.2 %all-gather = s32[16,1,1280]{2,1,0:T(1,128)S(1)} all-gather(s32[1,1,1280]{2,1,0:T(1,128)S(1)} %reshape.150), channel_id=1, replica_groups=mesh['ctx'=16,'head'=16] {'ctx'}, dimensions={0}, use_global_device_ids=true | all-gather | bytes 87040 | tf_op jit(solution)/shard_map/all_gather | solution.py:108
  118.7 4.7 %fusion.41 = f32[128,512]{1,0:T(8,128)S(1)} fusion(bf16[128,8192]{1,0:T(8,128)(2,1)S(1)} %copy-done, bf16[8192,512]{1,0:T(8,128)(2,1)} %param.10), kind=kOutput, calls=%fused_computation.64 | convolution fusion | flops 1073741824 | bytes 10747904 | tf_op jit(solution)/shard_map/dot_general | solution.py:57
  124.0 55.0 %all-gather.6.cloned.1.call-done = bf16[20480,256]{0,1:T(8,128)(2,1)} async-done(((bf16[1280,256]{0,1:T(8,128)(2,1)}), bf16[20480,256]{0,1:T(8,128)(2,1)}) %all-gather.6.cloned.1.call-update) | async-done | bytes 10485776 | tf_op jit(solution)/shard_map/all_gather | solution.py:107
  179.0 13.8 %copy.16 = bf16[20480,256]{1,0:T(8,128)(2,1)} copy(bf16[20480,256]{0,1:T(8,128)(2,1)} %all-gather.6.cloned.1.call-done) | data formatting | bytes 20971520 | tf_op jit(solution)/shard_map/all_gather | solution.py:107
  192.7 51.7 %while.15 = (s32[]{:T(128)}, f32[4,128]{1,0:T(4,128)S(1)}, f32[4,128]{1,0:T(4,128)S(1)}, f32[4,128,128]{2,1,0:T(8,128)S(1)}, s32[16,1280]{1,0:T(8,128)S(1)}, /*i...) while((s32[]{:T(128)}, f32[4,128]{1,0:T(4,128)S(1)}, ...), condition=%wide.region_3.4_spmd.clone, body=%wide.region_0.3_spmd.clone.sunk | while | flops 341150208 | bytes 11189889 | solution.py:114
  193.0 1.1 dynamic-slice_bitcast_fusion.2
  194.1 0.5 fusion.55
  195.2 0.7 fusion.58
  196.2 1.1 dynamic-slice_bitcast_fusion.2
  197.4 0.5 fusion.55
  198.4 0.7 fusion.58
  199.5 1.1 dynamic-slice_bitcast_fusion.2
  200.6 0.5 fusion.55
  201.6 0.7 fusion.58
  202.7 1.1 dynamic-slice_bitcast_fusion.2
  203.8 0.5 fusion.55
  204.9 0.7 fusion.58
  205.9 1.1 dynamic-slice_bitcast_fusion.2
  208.1 0.7 fusion.58
  209.2 1.1 dynamic-slice_bitcast_fusion.2
  211.3 0.7 fusion.58
  212.4 1.1 dynamic-slice_bitcast_fusion.2
  214.6 0.7 fusion.58
  215.6 1.1 dynamic-slice_bitcast_fusion.2
  217.8 0.7 fusion.58
  218.9 1.1 dynamic-slice_bitcast_fusion.2
  221.0 0.7 fusion.58
  222.1 1.1 dynamic-slice_bitcast_fusion.2
  224.3 0.7 fusion.58
  225.3 1.1 dynamic-slice_bitcast_fusion.2
  227.5 0.7 fusion.58
  228.6 1.1 dynamic-slice_bitcast_fusion.2
  230.7 0.7 fusion.58
  231.8 1.1 dynamic-slice_bitcast_fusion.2
  234.0 0.7 fusion.58
  235.0 1.1 dynamic-slice_bitcast_fusion.2
  237.2 0.7 fusion.58
  238.3 1.1 dynamic-slice_bitcast_fusion.2
  240.4 0.7 fusion.58
  241.5 1.1 dynamic-slice_bitcast_fusion.2
  243.7 0.7 fusion.58
  244.5 0.8 copy_bitcast_fusion
  (140 shorter events, 20.0 us)
Async XLA Ops:
  6.5 75.9 %all-gather.4.cloned.1.call-start = ((), (), s32[]{:S(2)}) async-start(), calls=%async_computation | async-start | bytes 2228224 | tf_op jit(solution)/shard_map/all_gather | solution.py:56
  7.3 78.3 %copy-start.1 = (bf16[1152,64]{0,1:T(8,128)(2,1)S(1)}, bf16[1152,64]{0,1:T(8,128)(2,1)}, u32[]{:S(2)}) copy-start(bf16[1152,64]{0,1:T(8,128)(2,1)} %param.14) | copy-start | bytes 442372
  7.3 78.3 %copy-start.2 = (bf16[1152,64]{0,1:T(8,128)(2,1)S(1)}, bf16[1152,64]{0,1:T(8,128)(2,1)}, u32[]{:S(2)}) copy-start(bf16[1152,64]{0,1:T(8,128)(2,1)} %param.13) | copy-start | bytes 442372
  7.3 79.7 %copy-start.3 = (s32[128]{0:T(128)S(1)}, s32[128]{0:T(128)}, u32[]{:S(2)}) copy-start(s32[128]{0:T(128)} %param.15) | copy-start | bytes 1540
  7.3 171.7 %all-gather.6.cloned.1.call-start = ((), (), s32[]{:S(2)}) async-start(), calls=%async_computation.1 | async-start | bytes 11141120 | tf_op jit(solution)/shard_map/all_gather | solution.py:107
  85.6 7.2 %collective-permute-start = (bf16[1280,128]{0,1:T(8,128)(2,1)S(1)}, bf16[1280,128]{0,1:T(8,128)(2,1)S(1)}, u32[]{:S(2)}, u32[]{:S(2)}) collective-permute-start(bf16[1280,128]{0,1:T(8,128)(2,1)S(1)} %pad_maximum_fusion.1), channel_id=1, source_target_pairs={{0,1},{1,0},{2,3},{3,2},{4,5},{5,4},{6,7},{7,6},{8,9},{9,8},{10,11... | collective-permute-start | bytes 983048 | tf_op jit(solution)/shard_map/ppermute | solution.py:19
  92.9 25.9 %copy-start = (bf16[128,8192]{1,0:T(8,128)(2,1)S(1)}, bf16[128,8192]{1,0:T(8,128)(2,1)}, u32[]{:S(2)}) copy-start(bf16[128,8192]{1,0:T(8,128)(2,1)} %all-gather.4.cloned.1.call-done) | copy-start | bytes 6291460
Sparse Core Ops, SparseCore 0:
  9.1 73.2 all-gather.3
  94.3 84.6 all-gather.5
where the time goes:
time: 255 us; the launch traced here: 252 us
  waiting for transfers between devices  137 us (54%)
  local copies, waits for them, and re-layouts  32.9 us (13%)
  matrix products  27.8 us (11%)
  blocking collectives  24.2 us (9%)
  other arithmetic  14.5 us (6%)
  between operations  13.6 us (5%)
    all_gather x1, waiting for transfers between devices, per_device(): piece = lax.all_gather(new_states, 'head', axis=1, tiled=True)  75.1 us
    all_gather x1, waiting for transfers between devices, per_device(): blocks = lax.all_gather(key_block, 'ctx', axis=0, tiled=True)  55 us
    all_gather x1, blocking collectives, per_device(): block_positions = lax.all_gather(key_positions, 'ctx', axis=0, tiled=True)  24.2 us
    squeeze x16, local copies, waits for them, and re-layouts, per_device(): running, _unused = lax.scan(stepper, running, stacked)  18.2 us
    all_gather x1, local copies, waits for them, and re-layouts, per_device(): blocks = lax.all_gather(key_block, 'ctx', axis=0, tiled=True)  13.8 us
    dot_general x16, matrix products, absorb_block(): jnp.einsum('hqk,kd->hqd', weights.astype(jnp.bfloat16), blocks[:, head_si...  12 us
    dot_general x16, matrix products, tile_scores(): jnp.einsum('qhd,kd->hqk', query_block, keys_here, preferred_element_type=...  8.19 us
    reduce_sum x16, other arithmetic, absorb_block(): weight_sum = weight_sum * factor + jnp.sum(weights, axis=2)  7.76 us
  transfers between devices with their start and end apart: 3, of which 3 were waited for; matrix products, arithmetic and copies ran while one was open for 2% of the time, Pallas kernels for 0%

commit v1 on v0

v1 whole, which is shorter than its diff:
```python
import math

import jax
import jax.numpy as jnp
from jax import lax
from jax.experimental import pallas as pl
from jax.experimental.pallas import tpu as pltpu
from jax.sharding import PartitionSpec as P

THETA = 500000.0
NEGATIVE = -1e30
MESH = pl.DeviceIdType.MESH
LOG2E = math.log2(math.e)

ROWS = 128
COLS = 512
HEAD = 128
HALF = 64
CACHE = 1152
QROWS = 512
SLOTS = 8
CUT = 128
SENDS = 64
NT = (((1,), (1,)), ((), ()))


def kernel(
    x_hbm, wq_hbm, wk_hbm, wv_hbm, ck_hbm, cv_hbm, pos_row, pos_col, cos_q, sin_q, cos_k, sin_k,
    out_ref,
    xbuf, wq, wkv, kvc, kvn, raw, qs, pos_far, q_sum, kv_sum, top, total, acc, o_out, o_in, st_out, st_in,
    local_sem, x_sem, kv_sem, kvn_sem, one_sem, send_sem,
):
    c = lax.axis_index("ctx")
    h = lax.axis_index("head")
    xh, yy, pp = c // 8, (c // 2) % 4, c % 2
    xl, z = h // 8, h % 8
    bit = h % 2
    away = 1 - bit

    def head_at(col, row):
        return col * 8 + (row + 8) % 8

    def ctx_at(row, core):
        return xh * 8 + ((row + 4) % 4) * 2 + core

    def slot_at(row, core):
        return ((row + 4) % 4) * 2 + core

    zp, zm = (c, head_at(xl, z + 1)), (c, head_at(xl, z - 1))
    xp = (c, head_at(1 - xl, z))
    pair = (c, h + 1 - 2 * bit)
    yp, ym = (ctx_at(yy + 1, pp), h), (ctx_at(yy - 1, pp), h)
    sib = (ctx_at(yy, 1 - pp), h)
    far = ((c + 8) % 16, h)
    mine = slot_at(yy, pp)

    pending = []

    def remote(src, dst, sem, device):
        copy = pltpu.make_async_remote_copy(
            src_ref=src, dst_ref=dst, send_sem=send_sem.at[len(pending)], recv_sem=sem,
            device_id=device, device_id_type=MESH,
        )
        pending.append(copy)
        copy.start()

    def arrived(ref, sem):
        pltpu.make_async_remote_copy(
            src_ref=ref, dst_ref=ref, send_sem=send_sem.at[0], recv_sem=sem,
            device_id=sib, device_id_type=MESH,
        ).wait_recv()

    def local(i, src, dst):
        copy = pltpu.make_async_copy(src, dst, local_sem.at[i])
        copy.start()
        return copy

    x_in = local(0, x_hbm, xbuf.at[h])
    k_in = local(1, ck_hbm, kvc.at[mine, bit, 0:HALF, :])
    v_in = local(2, cv_hbm, kvc.at[mine, bit, HALF:HEAD, :])
    wk_in = local(3, wk_hbm, wkv.at[0:HALF, :])
    wv_in = local(4, wv_hbm, wkv.at[HALF:HEAD, :])
    wq_in = [
        local(5 + i, wq_hbm.at[2048 * i : 2048 * (i + 1), :], wq.at[2048 * i : 2048 * (i + 1), :])
        for i in range(4)
    ]

    barrier = pltpu.get_barrier_semaphore()
    for device in (zp, zm, xp, yp, ym, sib, far):
        pl.semaphore_signal(barrier, inc=1, device_id=device, device_id_type=MESH)
    pl.semaphore_wait(barrier, 7)

    def piece(kind, slot):
        if kind == 0:
            return xbuf.at[slot, :, 0:CUT]
        return xbuf.at[slot, :, CUT:COLS]

    def send_x(kind, slot, device):
        remote(piece(kind, slot), piece(kind, slot), x_sem.at[kind, slot], device)

    def wait_x(kind, slot):
        arrived(piece(kind, slot), x_sem.at[kind, slot])

    def send_kv(slot, half, device):
        remote(kvc.at[slot, half], kvc.at[slot, half], kv_sem.at[slot, half], device)

    def wait_kv(slot, half):
        arrived(kvc.at[slot, half], kv_sem.at[slot, half])

    def send_new(slot, device):
        remote(kvn.at[slot], kvn.at[slot], kvn_sem.at[slot], device)

    def wait_new(slot):
        arrived(kvn.at[slot], kvn_sem.at[slot])

    x_in.wait()
    send_x(0, h, xp)
    for kind in (0, 1):
        send_x(kind, h, zp)
        send_x(kind, h, zm)
    send_x(1, h, xp)
    k_in.wait()
    v_in.wait()
    send_kv(mine, bit, pair)
    for device in (yp, ym, sib):
        send_kv(mine, bit, device)
    remote(pos_col, pos_far, one_sem.at[0], far)

    q_sum[...] = jnp.zeros_like(q_sum)
    kv_sum[...] = jnp.zeros_like(kv_sum)

    def project(slot):
        block = xbuf[slot]
        start = pl.multiple_of(slot * COLS, COLS)
        q_sum[...] += jnp.dot(block, wq[pl.ds(start, COLS), :], preferred_element_type=jnp.float32)
        kv_sum[...] += lax.dot_general(
            wkv[:, pl.ds(start, COLS)], block, NT, preferred_element_type=jnp.float32
        )

    reach = {(0, 1): 4, (0, -1): 3, (1, 1): 3, (1, -1): 4}

    def ring_step(t):
        for kind in (1, 0):
            for sign, ahead in ((1, zp), (-1, zm)):
                last = reach[kind, sign]
                if t > last:
                    continue
                slot = head_at(xl, z - sign * t)
                wait_x(kind, slot)
                if t < last:
                    send_x(kind, slot, ahead)
                if kind == 1:
                    send_x(1, slot, xp)
        if t == 1:
            slot = head_at(1 - xl, z)
            wait_x(0, slot)
            send_x(0, slot, zp)
            send_x(0, slot, zm)
        else:
            other_column(t - 1)

    def other_column(t):
        for sign, ahead in ((1, zp), (-1, zm)):
            last = reach[0, sign]
            if t > last:
                continue
            slot = head_at(1 - xl, z - sign * t)
            wait_x(0, slot)
            if t < last:
                send_x(0, slot, ahead)

    def other_rest(t):
        steps = (0,) if t == 0 else ((4,) if t == 4 else (t, -t))
        for step in steps:
            slot = head_at(1 - xl, z - step)
            wait_x(1, slot)
            project(slot)

    def own_column(t):
        steps = (0,) if t == 0 else ((4,) if t == 4 else (t, -t))
        for step in steps:
            project(head_at(xl, z - step))

    def kv_own_halves():
        wait_kv(mine, away)
        for device in (yp, ym, sib):
            send_kv(mine, away, device)

    def kv_from_sides(half):
        up, down = slot_at(yy - 1, pp), slot_at(yy + 1, pp)
        wait_kv(up, half)
        wait_kv(down, half)
        send_kv(slot_at(yy - 1 + 2 * half, pp), half, (ctx_at(yy + 1 - 2 * half, pp), h))
        send_kv(up, half, sib)
        send_kv(down, half, sib)

    ring_step(1)
    wk_in.wait()
    wv_in.wait()
    for copy in wq_in:
        copy.wait()
    own_column(0)
    ring_step(2)
    other_rest(0)
    own_column(1)
    kv_from_sides(bit)
    kv_own_halves()
    ring_step(3)
    other_rest(1)
    own_column(2)
    ring_step(4)
    other_column(4)
    other_rest(2)
    own_column(3)
    own_column(4)
    other_rest(3)
    other_rest(4)

    raw[bit] = kv_sum[...].astype(jnp.bfloat16)
    remote(raw.at[bit], raw.at[bit], one_sem.at[1], pair)
    cosine, sine = cos_q[...], sin_q[...]
    scale = HEAD**-0.5 * LOG2E
    for j in range(4):
        part = q_sum[:, HEAD * j : HEAD * (j + 1)]
        turned = part * cosine + pltpu.roll(part, HALF, 1) * sine
        qs[0, ROWS * j : ROWS * (j + 1), :] = (turned * scale).astype(jnp.bfloat16)
    remote(qs.at[0], qs.at[1], one_sem.at[2], far)

    arrived(raw.at[away], one_sem.at[1])
    lower, upper = raw[0].astype(jnp.float32), raw[1].astype(jnp.float32)
    low, high = lower[0:HALF], upper[0:HALF]
    cosine, sine = cos_k[...], sin_k[...]
    kvn[mine, 0:HALF, :] = (low * cosine - high * sine).astype(jnp.bfloat16)
    kvn[mine, HALF:HEAD, :] = (high * cosine + low * sine).astype(jnp.bfloat16)
    kvn[mine, HEAD : HEAD + HALF, :] = raw[0, HALF:HEAD, :]
    kvn[mine, HEAD + HALF : 2 * HEAD, :] = raw[1, HALF:HEAD, :]
    kvn[mine, 2 * HEAD :, :] = pos_row[...]
    for device in (yp, ym, sib):
        send_new(mine, device)

    top[...] = jnp.full_like(top, NEGATIVE)
    total[...] = jnp.zeros_like(total)
    acc[...] = jnp.zeros_like(acc)

    def attend(which, keys, values, hidden):
        scores = jnp.dot(qs[which], keys, preferred_element_type=jnp.float32)
        if hidden is not None:
            scores = jnp.where(hidden, NEGATIVE, scores)
        before = top[which, :, 0:1]
        now = jnp.maximum(before, jnp.max(scores, axis=1, keepdims=True))
        weights = jnp.exp2(scores - now)
        factor = jnp.exp2(before - now)
        total[which] = total[which] * factor + jnp.sum(weights, axis=1, keepdims=True)
        acc[which] = acc[which] * factor + lax.dot_general(
            weights.astype(jnp.bfloat16), values, NT, preferred_element_type=jnp.float32
        )
        top[which] = jnp.broadcast_to(now, (QROWS, HEAD))

    def attend_cached(which, slot):
        keys = jnp.concatenate([kvc[slot, 0, 0:HALF, :], kvc[slot, 1, 0:HALF, :]], axis=0)
        values = jnp.concatenate([kvc[slot, 0, HALF:HEAD, :], kvc[slot, 1, HALF:HEAD, :]], axis=0)
        attend(which, keys, values, None)

    def attend_new(which, where_ref):
        keys = jnp.concatenate([kvn[s, 0:HEAD, :] for s in range(SLOTS)], axis=1)
        values = jnp.concatenate([kvn[s, HEAD : 2 * HEAD, :] for s in range(SLOTS)], axis=1)
        code = jnp.concatenate([kvn[s, 2 * HEAD :, :] for s in range(SLOTS)], axis=1).astype(jnp.float32)
        key_pos = code[0:1] * 256.0 + code[1:2]
        code = where_ref[...].astype(jnp.float32)
        query_pos = code[:, 0:1] * 256.0 + code[:, 1:2]
        query_pos = jnp.concatenate([query_pos] * 4, axis=0)
        attend(which, keys, values, key_pos > query_pos)

    attend_cached(0, mine)
    kv_from_sides(away)
    wait_new(slot_at(yy - 1, pp))
    send_new(slot_at(yy - 1, pp), yp)
    send_new(slot_at(yy - 1, pp), sib)
    wait_new(slot_at(yy + 1, pp))
    send_new(slot_at(yy + 1, pp), sib)
    for core in (pp, 1 - pp):
        for row in (-1, 1):
            slot = slot_at(yy + row, core)
            if core is not pp:
                wait_kv(slot, 0)
                wait_kv(slot, 1)
            attend_cached(0, slot)
    opposite = slot_at(yy + 2, pp)
    wait_kv(opposite, 0)
    send_kv(opposite, 0, sib)
    wait_kv(opposite, 1)
    send_kv(opposite, 1, sib)
    wait_new(opposite)
    send_new(opposite, sib)
    wait_kv(slot_at(yy, 1 - pp), 0)
    wait_kv(slot_at(yy, 1 - pp), 1)
    attend_cached(0, slot_at(yy, 1 - pp))
    attend_cached(0, opposite)
    wait_kv(slot_at(yy + 2, 1 - pp), 0)
    wait_kv(slot_at(yy + 2, 1 - pp), 1)
    attend_cached(0, slot_at(yy + 2, 1 - pp))
    arrived(qs.at[1], one_sem.at[2])

    @pl.loop(0, SLOTS)
    def _(slot):
        attend_cached(1, slot)

    arrived(pos_far, one_sem.at[0])
    for row in (0, -1, 1, 2):
        wait_new(slot_at(yy + row, 1 - pp))
    attend_new(1, pos_far)
    o_out[...] = acc[1].astype(jnp.bfloat16)
    lane = lax.broadcasted_iota(jnp.int32, (ROWS, HEAD), 1)
    state = jnp.zeros((ROWS, HEAD), jnp.float32)
    for j in range(4):
        state = jnp.where(lane == j, top[1, ROWS * j : ROWS * (j + 1), :], state)
        state = jnp.where(lane == 4 + j, total[1, ROWS * j : ROWS * (j + 1), :], state)
    st_out[...] = state
    remote(st_out, st_in, one_sem.at[3], far)
    remote(o_out, o_in, one_sem.at[4], far)
    attend_new(0, pos_col)
    arrived(st_in, one_sem.at[3])
    arrived(o_in, one_sem.at[4])
    state = st_in[...]
    for j in range(4):
        rows = slice(ROWS * j, ROWS * (j + 1))
        here, there = top[0, rows, 0:1], state[:, j : j + 1]
        both = jnp.maximum(here, there)
        near_part, far_part = jnp.exp2(here - both), jnp.exp2(there - both)
        weight_sum = total[0, rows, 0:1] * near_part + state[:, 4 + j : 5 + j] * far_part
        mixed = acc[0, rows, :] * near_part + o_in[rows, :].astype(jnp.float32) * far_part
        out_ref[:, HEAD * j : HEAD * (j + 1)] = (mixed / weight_sum).astype(jnp.bfloat16)

    for copy in pending:
        copy.wait_send()


def per_device(
    new_states, query_weight, key_weight, value_weight, cache_keys, cache_values, new_positions
):
    inverse = jnp.exp(jnp.arange(HALF, dtype=jnp.float32) * (-2.0 * math.log(THETA) / HEAD))
    places = new_positions.astype(jnp.float32)
    angles = places[:, None] * inverse[None, :]
    cosine, sine = jnp.cos(angles), jnp.sin(angles)
    cos_q = jnp.concatenate([cosine, cosine], axis=1)
    sin_q = jnp.concatenate([-sine, sine], axis=1)
    turned = inverse[:, None] * places[None, :]
    cos_k, sin_k = jnp.cos(turned), jnp.sin(turned)
    coarse = (new_positions // 256).astype(jnp.bfloat16)
    fine = (new_positions % 256).astype(jnp.bfloat16)
    line = jnp.arange(16)[:, None]
    pos_row = jnp.where(line == 0, coarse[None, :], jnp.where(line == 1, fine[None, :], 0))
    line = jnp.arange(HEAD)[None, :]
    pos_col = jnp.where(line == 0, coarse[:, None], jnp.where(line == 1, fine[:, None], 0))

    hbm = pl.BlockSpec(memory_space=pl.ANY)
    vmem = pl.BlockSpec(memory_space=pltpu.VMEM)
    dma = pltpu.SemaphoreType.DMA
    bf16, f32 = jnp.bfloat16, jnp.float32
    return pl.pallas_call(
        kernel,
        out_shape=jax.ShapeDtypeStruct((ROWS, COLS), bf16),
        in_specs=[hbm] * 6 + [vmem] * 6,
        out_specs=vmem,
        scratch_shapes=[
            pltpu.VMEM((16, ROWS, COLS), bf16),
            pltpu.VMEM((8192, COLS), bf16),
            pltpu.VMEM((HEAD, 8192), bf16),
            pltpu.VMEM((SLOTS, 2, HEAD, CACHE), bf16),
            pltpu.VMEM((SLOTS, 2 * HEAD + 16, ROWS), bf16),
            pltpu.VMEM((2, HEAD, ROWS), bf16),
            pltpu.VMEM((2, QROWS, HEAD), bf16),
            pltpu.VMEM((ROWS, HEAD), bf16),
            pltpu.VMEM((ROWS, COLS), f32),
            pltpu.VMEM((HEAD, ROWS), f32),
            pltpu.VMEM((2, QROWS, HEAD), f32),
            pltpu.VMEM((2, QROWS, HEAD), f32),
            pltpu.VMEM((2, QROWS, HEAD), f32),
            pltpu.VMEM((QROWS, HEAD), bf16),
            pltpu.VMEM((QROWS, HEAD), bf16),
            pltpu.VMEM((ROWS, HEAD), f32),
            pltpu.VMEM((ROWS, HEAD), f32),
            dma((9,)),
            dma((2, 16)),
            dma((SLOTS, 2)),
            dma((SLOTS,)),
            dma((5,)),
            dma((SENDS,)),
        ],
        compiler_params=pltpu.CompilerParams(
            collective_id=0, has_side_effects=True, vmem_limit_bytes=56 << 20
        ),
    )(
        new_states, query_weight, key_weight.T, value_weight.T, cache_keys.T, cache_values.T,
        pos_row.astype(bf16), pos_col.astype(bf16), cos_q, sin_q, cos_k, sin_k,
    )


def solution(mesh):
    placed = (
        P("ctx", "head"),
        P(None, "head"),
        P(None, "head"),
        P(None, "head"),
        P("ctx", "head"),
        P("ctx", "head"),
        P("ctx"),
    )
    return jax.shard_map(
        per_device, mesh=mesh, in_specs=placed, out_specs=P("ctx", "head"), check_vma=False
    )
```

time: 255 us -> 82.1 us (0.32); the launches traced: 252 us -> 81.9 us
  waiting for transfers between devices: 137 us -> 0 us
  Pallas kernels: 0 us -> 76.3 us
  local copies, waits for them, and re-layouts: 32.9 us -> 1.57 us
  matrix products: 27.8 us -> 0 us
  blocking collectives: 24.2 us -> 0 us
  between operations: 13.6 us -> 0.02 us
  other arithmetic: 14.5 us -> 4.02 us
    all_gather x2 -> x0, waiting for transfers between devices: 130 us -> none  [the longest x1 75.1 us: per_device(): piece = lax.all_gather(new_states, 'head', axis=1, tiled=True)]
    pallas_call x0 -> x1, Pallas kernels: none -> 76.3 us  [per_device(): pl.pallas_call(kernel, out_shape=jax.ShapeDtypeStruct((ROWS, COLS), bf16)...]
    dot_general x34 -> x0, matrix products: 27.8 us -> none  [the longest x16 12 us: absorb_block(): jnp.einsum('hqk,kd->hqd', weights.astype(jnp.bfloat16), blocks[:, head_si...]
    all_gather x1 -> x0, blocking collectives: 24.2 us -> none  [per_device(): block_positions = lax.all_gather(key_positions, 'ctx', axis=0, tiled=True)]
    squeeze x16 -> x0, local copies, waits for them, and re-layouts: 18.2 us -> none  [per_device(): running, _unused = lax.scan(stepper, running, stacked)]
    all_gather x1 -> x0, local copies, waits for them, and re-layouts: 13.8 us -> none  [per_device(): blocks = lax.all_gather(key_block, 'ctx', axis=0, tiled=True)]
    reduce_sum x16 -> x0, other arithmetic: 7.76 us -> none  [absorb_block(): weight_sum = weight_sum * factor + jnp.sum(weights, axis=2)]
    ppermute x1 -> x0, waiting for transfers between devices: 5.78 us -> none  [swapped(): return lax.ppermute(block, axis, route)]
  transfers between devices with their start and end apart: 3 -> 0, of which waited for: 3 -> 0; matrix products, arithmetic and copies ran while one was open for 2% -> 0% of each run, Pallas kernels for 0% -> 0%
where the time goes in v1:
time: 82.1 us; the launch traced here: 81.9 us
  Pallas kernels  76.3 us (93%)
  other arithmetic  4.02 us (5%)
  local copies, waits for them, and re-layouts  1.57 us (2%)
    pallas_call x1, Pallas kernels, per_device(): pl.pallas_call(kernel, out_shape=jax.ShapeDtypeStruct((ROWS, COLS), bf16)...  76.3 us

profile of v1, /device:TPU:32, one launch (start us, length us, event | category | flops | bytes accessed | tf_op | source)
XLA Modules:
  0.0 81.9 jit_solution(5048929361462166286)
XLA Ops:
  0.0 0.7 fusion.3
  0.8 0.3 fusion
  1.1 0.8 pad_maximum_fusion
  1.8 0.7 select_select_fusion.pos_col
  2.5 0.7 select_select_fusion.1.pos_row
  3.2 0.8 %multiply_sine_fusion.1 = (f32[64,128]{1,0:T(8,128)}, f32[64,128]{1,0:T(8,128)}) fusion(f32[128]{0:T(128)S(1)} %get-tuple-element.10, f32[64]{0:T(128)S(1)} %multiply_exponential_fusion), kind=kLoop, calls=%fused_computation.4 | loop fusion | flops 8192 | bytes 66304 | tf_op jit(solution)/shard_map/sin | solution.py:348
  4.0 76.3 %shard_map.73 = bf16[128,512]{1,0:T(8,128)(2,1)} custom-call(bf16[128,512]{1,0:T(8,128)(2,1)} %x_hbm.1, bf16[8192,512]{1,0:T(8,128)(2,1)} %wq_hbm.1, bf16[64,8192]{1,0:T(8,128)(2,1)} %bitcast.4, bf16[64,8192]{1,0:T(8,128)(2,1)} %bitcast.5, bf16[64,1152]{1,0:T(8,128)(2,1)} %bitcast.6, bf16[64,1152]{1,0:T(8,128)(2,1)} %bitcast.7, ...), custom_call_target="tpu_custom_call" | custom-call | tf_op jit(solution)/shard_map/pallas_call | solution.py:360
  80.3 1.6 %copy.9 = bf16[128,512]{1,0:T(8,128)(2,1)} copy(bf16[128,512]{1,0:T(8,128)(2,1)} %shard_map.73) | data formatting | bytes 262144
  (3 shorter events, 0.0 us)

commit v2 on v1

v2 whole, which is shorter than its diff:
```python
import math

import jax
import jax.numpy as jnp
import numpy as np
from jax import lax
from jax.experimental import pallas as pl
from jax.experimental.pallas import tpu as pltpu
from jax.sharding import PartitionSpec as P

THETA = 500000.0
NEGATIVE = -1e30
MESH = pl.DeviceIdType.MESH
LOG2E = math.log2(math.e)

ROWS = 128
COLS = 512
HEAD = 128
HALF = 64
CACHE = 1152
QROWS = 512
PART = 256
LINES = 4
SENDS = 96
CUTS = ((0, 128), (128, 384), (384, 512))
REACH = {(0, 1): 4, (0, -1): 3, (1, 1): 3, (1, -1): 4, (2, 1): 4, (2, -1): 3}
NT = (((1,), (1,)), ((), ()))


def kernel(
    x_hbm, wq_hbm, wk_hbm, wv_hbm, ck_hbm, cv_hbm, pos_ref, turn_ref,
    out_ref,
    xbuf, wq, wkv, kvc, kvn, raw, qs, places, q_sum, kv_sum, top, total, acc, sbuf, nbuf,
    cos_q, sin_q, cos_k, sin_k, query_pos, o_out, o_in, st_out, st_in,
    local_sem, x_sem, kv_sem, kvn_sem, one_sem, send_sem,
):
    c = lax.axis_index("ctx")
    h = lax.axis_index("head")
    xh, yy, pp = c // 8, (c // 2) % 4, c % 2
    xl, z = h // 8, h % 8
    bit = h % 2
    away = 1 - bit
    other = 1 - pp

    def head_at(col, row):
        return col * 8 + (row + 8) % 8

    def ctx_at(row, core):
        return xh * 8 + ((row + 4) % 4) * 2 + core

    def line(step):
        return (yy + step + 4) % 4

    zp, zm = (c, head_at(xl, z + 1)), (c, head_at(xl, z - 1))
    xp = (c, head_at(1 - xl, z))
    pair = (c, h + 1 - 2 * bit)
    yp, ym = (ctx_at(yy + 1, pp), h), (ctx_at(yy - 1, pp), h)
    sib = (ctx_at(yy, other), h)
    far = ((c + 8) % 16, h)

    pending = []

    def remote(src, dst, sem, device, like=None):
        number = len(pending)
        pltpu.make_async_remote_copy(
            src_ref=src, dst_ref=dst, send_sem=send_sem.at[number], recv_sem=sem,
            device_id=device, device_id_type=MESH,
        ).start()
        pending.append(like or (lambda: src))

    def arrived(ref, sem):
        pltpu.make_async_remote_copy(
            src_ref=ref, dst_ref=ref, send_sem=send_sem.at[0], recv_sem=sem,
            device_id=sib, device_id_type=MESH,
        ).wait_recv()

    def local(i, src, dst):
        copy = pltpu.make_async_copy(src, dst, local_sem.at[i])
        copy.start()
        return copy

    def cached(row, half, core):
        return kvc.at[row, half, :, pl.ds(pl.multiple_of(core * CACHE, 128), CACHE)]

    own = pl.ds(pl.multiple_of(pp * CACHE, 128), CACHE)
    x_in = local(0, x_hbm, xbuf.at[h])
    k_in = local(1, ck_hbm, kvc.at[yy, bit, 0:HALF, own])
    v_in = local(2, cv_hbm, kvc.at[yy, bit, HALF:HEAD, own])
    wk_in = local(3, wk_hbm, wkv.at[0:HALF, :])
    wv_in = local(4, wv_hbm, wkv.at[HALF:HEAD, :])
    wq_in = [
        local(5 + i, wq_hbm.at[2048 * i : 2048 * (i + 1), :], wq.at[2048 * i : 2048 * (i + 1), :])
        for i in range(4)
    ]

    barrier = pltpu.get_barrier_semaphore()
    for device in (zp, zm, xp, yp, ym, sib, far):
        pl.semaphore_signal(barrier, inc=1, device_id=device, device_id_type=MESH)

    position = pos_ref[...]
    row_index = lax.broadcasted_iota(jnp.int32, (16, ROWS), 0)
    coarse = jnp.broadcast_to((position // 256).astype(jnp.float32), (16, ROWS))
    fine = jnp.broadcast_to((position % 256).astype(jnp.float32), (16, ROWS))
    places[0] = jnp.where(row_index == 0, coarse, jnp.where(row_index == 1, fine, 0.0)).astype(jnp.bfloat16)
    kvn[yy * 2 + pp, 2 * HEAD :, :] = places[0]
    pl.semaphore_wait(barrier, 7)

    def piece(kind, slot):
        return xbuf.at[slot, :, CUTS[kind][0] : CUTS[kind][1]]

    def send_x(kind, slot, device):
        remote(piece(kind, slot), piece(kind, slot), x_sem.at[kind, slot], device)

    def wait_x(kind, slot):
        arrived(piece(kind, slot), x_sem.at[kind, slot])

    def send_kv(row, half, core, device):
        block = cached(row, half, core)
        remote(block, block, kv_sem.at[row, half, core], device, lambda: kvc.at[0, 0, :, 0:CACHE])

    def wait_kv(row, half, core):
        arrived(cached(row, half, core), kv_sem.at[row, half, core])

    def send_new(row, core, device):
        slot = row * 2 + core
        remote(kvn.at[slot], kvn.at[slot], kvn_sem.at[slot], device, lambda: kvn.at[0])

    def wait_new(row, core):
        slot = row * 2 + core
        arrived(kvn.at[slot], kvn_sem.at[slot])

    across = head_at(1 - xl, z)

    def first_wave():
        x_in.wait()
        send_x(0, h, xp)
        for kind in (1, 0):
            send_x(kind, h, zp)
            send_x(kind, h, zm)
        send_x(1, h, xp)

    def second_wave():
        send_x(2, h, zp)
        send_x(2, h, zm)
        send_x(2, h, xp)
        wait_x(0, across)
        send_x(0, across, zp)
        send_x(0, across, zm)

    def ring(t, kind, col):
        for sign, ahead in ((1, zp), (-1, zm)):
            last = REACH[kind, sign]
            if t > last:
                continue
            slot = head_at(col, z - sign * t)
            wait_x(kind, slot)
            if t < last:
                send_x(kind, slot, ahead)
            if kind > 0:
                send_x(kind, slot, xp)

    def ring_step(t):
        ring(t, 1, xl)
        ring(t, 0, xl)
        ring(t, 2, xl)
        ring(t, 0, 1 - xl)

    def project(slot):
        block = xbuf[slot]
        start = pl.multiple_of(slot * COLS, COLS)
        q_sum[...] += jnp.dot(block, wq[pl.ds(start, COLS), :], preferred_element_type=jnp.float32)
        kv_sum[...] += lax.dot_general(
            wkv[:, pl.ds(start, COLS)], block, NT, preferred_element_type=jnp.float32
        )

    def steps(t):
        return (0,) if t == 0 else ((4,) if t == 4 else (t, -t))

    def own_column(t):
        for step in steps(t):
            project(head_at(xl, z - step))

    def other_column(t):
        for step in steps(t):
            slot = head_at(1 - xl, z - step)
            wait_x(1, slot)
            wait_x(2, slot)
            project(slot)

    def kv_start():
        k_in.wait()
        v_in.wait()
        for device in (yp, ym, sib):
            send_kv(yy, bit, pp, device)

    def kv_pair():
        send_kv(yy, bit, pp, pair)

    def kv_own_halves():
        wait_kv(yy, away, pp)
        for device in (yp, ym, sib):
            send_kv(yy, away, pp, device)

    def kv_forward(half):
        step = 2 * half - 1
        wait_kv(line(step), half, pp)
        send_kv(line(step), half, pp, (ctx_at(yy - step, pp), h))
        send_kv(line(step), half, pp, sib)

    def kv_rest(half):
        step = 1 - 2 * half
        wait_kv(line(step), half, pp)
        send_kv(line(step), half, pp, sib)

    def kv_opposite(half):
        wait_kv(line(2), half, pp)
        send_kv(line(2), half, pp, sib)

    def tables():
        angles = turn_ref[...] * position.astype(jnp.float32)
        cosine, sine = jnp.cos(angles), jnp.sin(angles)
        cos_k[...] = cosine
        sin_k[...] = sine
        cos_q[...] = jnp.concatenate([cosine, cosine], axis=0).T
        sin_q[...] = jnp.concatenate([-sine, sine], axis=0).T
        query_pos[0] = jnp.broadcast_to(position.astype(jnp.float32), (ROWS, ROWS)).T
        q_sum[...] = jnp.zeros_like(q_sum)
        kv_sum[...] = jnp.zeros_like(kv_sum)
        top[...] = jnp.full_like(top, NEGATIVE)
        total[...] = jnp.zeros_like(total)
        acc[...] = jnp.zeros_like(acc)

    first_wave()
    kv_start()
    remote(places.at[0], places.at[1], one_sem.at[0], far)
    second_wave()
    tables()
    ring_step(1)
    wk_in.wait()
    wv_in.wait()
    for copy in wq_in:
        copy.wait()
    own_column(0)
    ring_step(2)
    kv_pair()
    kv_forward(bit)
    kv_rest(bit)
    other_column(0)
    own_column(1)
    ring_step(3)
    other_column(1)
    own_column(2)
    ring_step(4)
    kv_own_halves()
    other_column(2)
    own_column(3)
    own_column(4)
    other_column(3)
    other_column(4)

    raw[bit] = kv_sum[...].astype(jnp.bfloat16)
    remote(raw.at[bit], raw.at[bit], one_sem.at[1], pair)
    cosine, sine = cos_q[...], sin_q[...]
    scale = HEAD**-0.5 * LOG2E
    for j in range(4):
        part = q_sum[:, HEAD * j : HEAD * (j + 1)]
        turned = part * cosine + pltpu.roll(part, HALF, 1) * sine
        qs[0, ROWS * j : ROWS * (j + 1), :] = (turned * scale).astype(jnp.bfloat16)
    remote(qs.at[0], qs.at[1], one_sem.at[2], far)

    def new_rows():
        arrived(raw.at[away], one_sem.at[1])
        low, high = raw[0, 0:HALF, :].astype(jnp.float32), raw[1, 0:HALF, :].astype(jnp.float32)
        cosine, sine = cos_k[...], sin_k[...]
        slot = yy * 2 + pp
        kvn[slot, 0:HALF, :] = (low * cosine - high * sine).astype(jnp.bfloat16)
        kvn[slot, HALF:HEAD, :] = (high * cosine + low * sine).astype(jnp.bfloat16)
        kvn[slot, HEAD : HEAD + HALF, :] = raw[0, HALF:HEAD, :]
        kvn[slot, HEAD + HALF : 2 * HEAD, :] = raw[1, HALF:HEAD, :]
        for device in (yp, ym, sib):
            send_new(yy, pp, device)

    def new_from_sides():
        wait_new(line(-1), pp)
        send_new(line(-1), pp, yp)
        send_new(line(-1), pp, sib)
        wait_new(line(1), pp)
        send_new(line(1), pp, sib)

    def new_opposite():
        wait_new(line(2), pp)
        send_new(line(2), pp, sib)

    def soften(which, r, tiles, values):
        rows = slice(PART * r, PART * (r + 1))
        before = top[which, rows]
        highest = tiles[0]
        for tile in tiles[1:]:
            highest = jnp.maximum(highest, tile)
        now = jnp.maximum(before, jnp.max(highest, axis=1, keepdims=True))
        factor = jnp.exp2(before - now)
        weights = [jnp.exp2(tile - now) for tile in tiles]
        added = weights[0]
        for weight in weights[1:]:
            added = added + weight
        total[which, rows] = total[which, rows] * factor + added
        top[which, rows] = now
        packed = jnp.concatenate([weight.astype(jnp.bfloat16) for weight in weights], axis=1)
        acc[which, rows] = acc[which, rows] * factor + lax.dot_general(
            packed, values, NT, preferred_element_type=jnp.float32
        )

    def split(scores):
        return [scores[:, 128 * j : 128 * (j + 1)] for j in range(scores.shape[1] // 128)]

    def scores(which, row, r):
        keys = jnp.concatenate([kvc[row, 0, 0:HALF, :], kvc[row, 1, 0:HALF, :]], axis=0)
        return jnp.dot(qs[which, PART * r : PART * (r + 1), :], keys, preferred_element_type=jnp.float32)

    def cached_values(row):
        return jnp.concatenate([kvc[row, 0, HALF:HEAD, :], kvc[row, 1, HALF:HEAD, :]], axis=0)

    def job(i):
        late = i // 4
        which = (1 - late) * (i % 2) + late * (1 - i % 4 // 2)
        return which, line((1 - late) * (i // 2) + late * (3 - i % 2))

    def new_scores(which, r):
        keys = jnp.concatenate([kvn[s, 0:HEAD, :] for s in range(2 * LINES)], axis=1)
        return jnp.dot(qs[which, PART * r : PART * (r + 1), :], keys, preferred_element_type=jnp.float32)

    def soften_new(which, r, found):
        asked = jnp.concatenate([query_pos[which]] * (PART // ROWS), axis=0)
        tiles = []
        for s, tile in enumerate(split(found)):
            code = kvn[s, 2 * HEAD :, :].astype(jnp.float32)
            tiles.append(jnp.where(code[0:1] * 256.0 + code[1:2] <= asked, tile, NEGATIVE))
        values = jnp.concatenate([kvn[s, HEAD : 2 * HEAD, :] for s in range(2 * LINES)], axis=1)
        soften(which, r, tiles, values)

    kv_opposite(bit)
    for half in (0, 1):
        wait_kv(yy, half, other)
    sbuf[0] = scores(0, yy, 0)

    @pl.loop(0, 6)
    def _(i):
        @pl.when(i == 0)
        def _():
            new_rows()
            kv_forward(away)
            arrived(qs.at[1], one_sem.at[2])

        @pl.when(i == 1)
        def _():
            kv_rest(away)
            for half in (0, 1):
                wait_kv(line(1), half, other)

        @pl.when(i == 2)
        def _():
            new_from_sides()

        @pl.when(i == 3)
        def _():
            kv_opposite(away)
            for half in (0, 1):
                wait_kv(line(3), half, other)

        @pl.when(i == 4)
        def _():
            new_opposite()
            for half in (0, 1):
                wait_kv(line(2), half, other)

        which, row = job(i)
        found = sbuf[0]
        sbuf[1] = scores(which, row, 1)
        values = cached_values(row)
        soften(which, 0, split(found), values)
        found = sbuf[1]
        next_which, next_row = job(i + 1)
        sbuf[0] = scores(next_which, next_row, 0)
        soften(which, 1, split(found), values)

    arrived(places.at[1], one_sem.at[0])
    code = places[1].astype(jnp.float32)
    query_pos[1] = jnp.broadcast_to(code[0:1] * 256.0 + code[1:2], (ROWS, ROWS)).T
    for step in range(LINES):
        wait_new(line(step), other)
    nbuf[0] = new_scores(1, 0)
    nbuf[1] = new_scores(1, 1)
    soften_new(1, 0, nbuf[0])
    soften_new(1, 1, nbuf[1])
    o_out[...] = acc[1].astype(jnp.bfloat16)
    lane = lax.broadcasted_iota(jnp.int32, (ROWS, HEAD), 1)
    state = jnp.zeros((ROWS, HEAD), jnp.float32)
    for j in range(4):
        rows = slice(ROWS * j, ROWS * (j + 1))
        state = jnp.where(lane == j, top[1, rows, :], state)
        state = jnp.where(lane == 4 + j, jnp.sum(total[1, rows, :], axis=1, keepdims=True), state)
    st_out[...] = state
    remote(st_out, st_in, one_sem.at[3], far)
    remote(o_out, o_in, one_sem.at[4], far)

    nbuf[0] = new_scores(0, 0)
    nbuf[1] = new_scores(0, 1)
    for i in (6, 7):
        which, row = 0, line(9 - i)
        found = sbuf[0]
        sbuf[1] = scores(which, row, 1)
        values = cached_values(row)
        soften(which, 0, split(found), values)
        found = sbuf[1]
        if i == 6:
            sbuf[0] = scores(0, line(2), 0)
        soften(which, 1, split(found), values)
    soften_new(0, 0, nbuf[0])
    soften_new(0, 1, nbuf[1])

    arrived(st_in, one_sem.at[3])
    arrived(o_in, one_sem.at[4])
    state = st_in[...]
    for j in range(4):
        rows = slice(ROWS * j, ROWS * (j + 1))
        here, there = top[0, rows, :], state[:, j : j + 1]
        both = jnp.maximum(here, there)
        near_part, far_part = jnp.exp2(here - both), jnp.exp2(there - both)
        near_sum = jnp.sum(total[0, rows, :], axis=1, keepdims=True)
        weight_sum = near_sum * near_part + state[:, 4 + j : 5 + j] * far_part
        mixed = acc[0, rows, :] * near_part + o_in[rows, :].astype(jnp.float32) * far_part
        out_ref[:, HEAD * j : HEAD * (j + 1)] = (mixed / weight_sum).astype(jnp.bfloat16)

    for number, like in enumerate(pending):
        ref = like()
        pltpu.make_async_remote_copy(
            src_ref=ref, dst_ref=ref, send_sem=send_sem.at[number], recv_sem=one_sem.at[0],
            device_id=sib, device_id_type=MESH,
        ).wait_send()


def per_device(
    new_states, query_weight, key_weight, value_weight, cache_keys, cache_values, new_positions
):
    turn = THETA ** (np.arange(HALF) * (-2.0 / HEAD))
    turn = jnp.asarray(np.repeat(turn[:, None], ROWS, axis=1), jnp.float32)
    hbm = pl.BlockSpec(memory_space=pl.ANY)
    vmem = pl.BlockSpec(memory_space=pltpu.VMEM)
    dma = pltpu.SemaphoreType.DMA
    bf16, f32 = jnp.bfloat16, jnp.float32
    scratch = [
        ((16, ROWS, COLS), bf16),
        ((8192, COLS), bf16),
        ((HEAD, 8192), bf16),
        ((LINES, 2, HEAD, 2 * CACHE), bf16),
        ((2 * LINES, 2 * HEAD + 16, ROWS), bf16),
        ((2, HEAD, ROWS), bf16),
        ((2, QROWS, HEAD), bf16),
        ((2, 16, ROWS), bf16),
        ((ROWS, COLS), f32),
        ((HEAD, ROWS), f32),
        ((2, QROWS, HEAD), f32),
        ((2, QROWS, HEAD), f32),
        ((2, QROWS, HEAD), f32),
        ((2, PART, 2 * CACHE), f32),
        ((2, PART, 2 * LINES * ROWS), f32),
        ((ROWS, HEAD), f32),
        ((ROWS, HEAD), f32),
        ((HALF, ROWS), f32),
        ((HALF, ROWS), f32),
        ((2, ROWS, HEAD), f32),
        ((QROWS, HEAD), bf16),
        ((QROWS, HEAD), bf16),
        ((ROWS, HEAD), f32),
        ((ROWS, HEAD), f32),
    ]
    return pl.pallas_call(
        kernel,
        out_shape=jax.ShapeDtypeStruct((ROWS, COLS), bf16),
        in_specs=[hbm] * 6 + [vmem] * 2,
        out_specs=vmem,
        scratch_shapes=[pltpu.VMEM(shape, kind) for shape, kind in scratch]
        + [dma((9,)), dma((3, 16)), dma((LINES, 2, 2)), dma((2 * LINES,)), dma((5,)), dma((SENDS,))],
        compiler_params=pltpu.CompilerParams(
            collective_id=0, has_side_effects=True, vmem_limit_bytes=56 << 20
        ),
    )(
        new_states, query_weight, key_weight.T, value_weight.T, cache_keys.T, cache_values.T,
        new_positions.reshape(1, ROWS), turn,
    )


def solution(mesh):
    placed = (
        P("ctx", "head"),
        P(None, "head"),
        P(None, "head"),
        P(None, "head"),
        P("ctx", "head"),
        P("ctx", "head"),
        P("ctx"),
    )
    return jax.shard_map(
        per_device, mesh=mesh, in_specs=placed, out_specs=P("ctx", "head"), check_vma=False
    )
```

time: 82.1 us -> 62.3 us (0.76)
  Pallas kernels: 76.3 us -> 60.3 us
  other arithmetic: 4.02 us -> 0 us
    pallas_call x1, Pallas kernels: 76.3 us -> 60.3 us  [per_device(): pl.pallas_call(kernel, out_shape=jax.ShapeDtypeStruct((ROWS, COLS), bf16)...]
    select_n x2 -> x0, other arithmetic: 1.37 us -> none  [the longest x1 0.71 us: per_device(): jnp.where(line == 0, coarse[:, None], jnp.where(line == 1, fine[:, None],...]
    sin x1 -> x0, other arithmetic: 0.83 us -> none  [per_device(): cos_k, sin_k = (jnp.cos(turned), jnp.sin(turned))]
where the time goes in v2:
time: 62.3 us; the launch traced here: 61.9 us
  Pallas kernels  60.3 us (97%)
  local copies, waits for them, and re-layouts  1.57 us (3%)
    pallas_call x1, Pallas kernels, per_device(): pl.pallas_call(kernel, out_shape=jax.ShapeDtypeStruct((ROWS, COLS), bf16)...  60.3 us
    unnamed x1, local copies, waits for them, and re-layouts  1.57 us

profile of v2, /device:TPU:32, one launch (start us, length us, event | category | flops | bytes accessed | tf_op | source)
XLA Modules:
  0.0 61.9 jit_solution(5806949076830490750)
XLA Ops:
  0.0 60.3 %shard_map.82 = bf16[128,512]{1,0:T(8,128)(2,1)} custom-call(bf16[128,512]{1,0:T(8,128)(2,1)} %x_hbm.1, bf16[8192,512]{1,0:T(8,128)(2,1)} %wq_hbm.1, bf16[64,8192]{1,0:T(8,128)(2,1)} %bitcast.5, bf16[64,8192]{1,0:T(8,128)(2,1)} %bitcast.6, bf16[64,1152]{1,0:T(8,128)(2,1)} %bitcast.7, bf16[64,1152]{1,0:T(8,128)(2,1)} %bitcast.8, s32[1,128]{1,0:T(1,128)} %bitcast.9, ...), custom_call_target="tpu_custom_call" | custom-call | tf_op jit(solution)/shard_map/pallas_call | solution.py:477
  60.3 1.6 %copy.10 = bf16[128,512]{1,0:T(8,128)(2,1)} copy(bf16[128,512]{1,0:T(8,128)(2,1)} %shard_map.82) | data formatting | bytes 262144

commit v3 on v2

--- a/solution.py
+++ b/solution.py
@@ -21,7 +21,9 @@
 QROWS = 512
 PART = 256
 LINES = 4
-SENDS = 96
+SENDS = 120
+CHUNKS = 3
+CHUNK = 384
 CUTS = ((0, 128), (128, 384), (384, 512))
 REACH = {(0, 1): 4, (0, -1): 3, (1, 1): 3, (1, -1): 4, (2, 1): 4, (2, -1): 3}
 NT = (((1,), (1,)), ((), ()))
@@ -79,8 +81,8 @@
         copy.start()
         return copy
 
-    def cached(row, half, core):
-        return kvc.at[row, half, :, pl.ds(pl.multiple_of(core * CACHE, 128), CACHE)]
+    def cached(row, half, core, k):
+        return kvc.at[row, half, :, pl.ds(pl.multiple_of(core * CACHE + k * CHUNK, 128), CHUNK)]
 
     own = pl.ds(pl.multiple_of(pp * CACHE, 128), CACHE)
     x_in = local(0, x_hbm, xbuf.at[h])
@@ -114,12 +116,17 @@
     def wait_x(kind, slot):
         arrived(piece(kind, slot), x_sem.at[kind, slot])
 
-    def send_kv(row, half, core, device):
-        block = cached(row, half, core)
-        remote(block, block, kv_sem.at[row, half, core], device, lambda: kvc.at[0, 0, :, 0:CACHE])
-
-    def wait_kv(row, half, core):
-        arrived(cached(row, half, core), kv_sem.at[row, half, core])
+    def send_kv(row, half, core, k, device):
+        block = cached(row, half, core, k)
+        remote(block, block, kv_sem.at[row, half, core * CHUNKS + k], device, lambda: kvc.at[0, 0, :, 0:CHUNK])
+
+    def wait_kv(row, half, core, k):
+        arrived(cached(row, half, core, k), kv_sem.at[row, half, core * CHUNKS + k])
+
+    def wait_row(row):
+        for half in (0, 1):
+            for k in range(CHUNKS):
+                wait_kv(row, half, other, k)
 
     def send_new(row, core, device):
         slot = row * 2 + core
@@ -190,31 +197,32 @@
     def kv_start():
         k_in.wait()
         v_in.wait()
+        for k in range(CHUNKS):
+            for device in (yp, ym, sib):
+                send_kv(yy, bit, pp, k, device)
+
+    def kv_pair(k):
+        send_kv(yy, bit, pp, k, pair)
+
+    def kv_own_halves(k):
+        wait_kv(yy, away, pp, k)
         for device in (yp, ym, sib):
-            send_kv(yy, bit, pp, device)
-
-    def kv_pair():
-        send_kv(yy, bit, pp, pair)
-
-    def kv_own_halves():
-        wait_kv(yy, away, pp)
-        for device in (yp, ym, sib):
-            send_kv(yy, away, pp, device)
-
-    def kv_forward(half):
+            send_kv(yy, away, pp, k, device)
+
+    def kv_forward(half, k):
         step = 2 * half - 1
-        wait_kv(line(step), half, pp)
-        send_kv(line(step), half, pp, (ctx_at(yy - step, pp), h))
-        send_kv(line(step), half, pp, sib)
-
-    def kv_rest(half):
+        wait_kv(line(step), half, pp, k)
+        send_kv(line(step), half, pp, k, (ctx_at(yy - step, pp), h))
+        send_kv(line(step), half, pp, k, sib)
+
+    def kv_rest(half, k):
         step = 1 - 2 * half
-        wait_kv(line(step), half, pp)
-        send_kv(line(step), half, pp, sib)
-
-    def kv_opposite(half):
-        wait_kv(line(2), half, pp)
-        send_kv(line(2), half, pp, sib)
+        wait_kv(line(step), half, pp, k)
+        send_kv(line(step), half, pp, k, sib)
+
+    def kv_opposite(half, k):
+        wait_kv(line(2), half, pp, k)
+        send_kv(line(2), half, pp, k, sib)
 
     def tables():
         angles = turn_ref[...] * position.astype(jnp.float32)
@@ -234,24 +242,33 @@
     kv_start()
     remote(places.at[0], places.at[1], one_sem.at[0], far)
     second_wave()
+    kv_pair(0)
     tables()
     ring_step(1)
+    kv_pair(1)
     wk_in.wait()
     wv_in.wait()
     for copy in wq_in:
         copy.wait()
     own_column(0)
     ring_step(2)
-    kv_pair()
-    kv_forward(bit)
-    kv_rest(bit)
+    kv_pair(2)
+    kv_own_halves(0)
+    for k in range(CHUNKS):
+        kv_forward(bit, k)
+    for k in range(CHUNKS):
+        kv_rest(bit, k)
     other_column(0)
     own_column(1)
     ring_step(3)
+    kv_own_halves(1)
+    kv_forward(away, 0)
     other_column(1)
     own_column(2)
     ring_step(4)
-    kv_own_halves()
+    kv_own_halves(2)
+    kv_forward(away, 1)
+    kv_rest(away, 0)
     other_column(2)
     own_column(3)
     own_column(4)
@@ -321,9 +338,10 @@
         return jnp.concatenate([kvc[row, 0, HALF:HEAD, :], kvc[row, 1, HALF:HEAD, :]], axis=0)
 
     def job(i):
-        late = i // 4
-        which = (1 - late) * (i % 2) + late * (1 - i % 4 // 2)
-        return which, line((1 - late) * (i // 2) + late * (3 - i % 2))
+        which = (i + 3) // 4 % 2
+        turn = (i + 3) % 4 * which + i // 5
+        step = turn * (1 - turn // 2) + turn // 2 * (5 - turn)
+        return which, line(step)
 
     def new_scores(which, r):
         keys = jnp.concatenate([kvn[s, 0:HEAD, :] for s in range(2 * LINES)], axis=1)
@@ -338,40 +356,36 @@
         values = jnp.concatenate([kvn[s, HEAD : 2 * HEAD, :] for s in range(2 * LINES)], axis=1)
         soften(which, r, tiles, values)
 
-    kv_opposite(bit)
-    for half in (0, 1):
-        wait_kv(yy, half, other)
+    for k in range(CHUNKS):
+        kv_opposite(bit, k)
+    wait_row(yy)
     sbuf[0] = scores(0, yy, 0)
 
-    @pl.loop(0, 6)
+    @pl.loop(0, 5)
     def _(i):
         @pl.when(i == 0)
         def _():
             new_rows()
-            kv_forward(away)
+            kv_forward(away, 2)
+            kv_rest(away, 1)
             arrived(qs.at[1], one_sem.at[2])
 
         @pl.when(i == 1)
         def _():
-            kv_rest(away)
-            for half in (0, 1):
-                wait_kv(line(1), half, other)
+            kv_rest(away, 2)
+            wait_row(line(1))
+            new_from_sides()
 
         @pl.when(i == 2)
         def _():
-            new_from_sides()
+            for k in range(CHUNKS):
+                kv_opposite(away, k)
+            wait_row(line(3))
 
         @pl.when(i == 3)
         def _():
-            kv_opposite(away)
-            for half in (0, 1):
-                wait_kv(line(3), half, other)
-
-        @pl.when(i == 4)
-        def _():
             new_opposite()
-            for half in (0, 1):
-                wait_kv(line(2), half, other)
+            wait_row(line(2))
 
         which, row = job(i)
         found = sbuf[0]
@@ -405,15 +419,15 @@
 
     nbuf[0] = new_scores(0, 0)
     nbuf[1] = new_scores(0, 1)
-    for i in (6, 7):
-        which, row = 0, line(9 - i)
+    for i, step in ((5, 1), (6, 3), (7, 2)):
+        which, row = 0, line(step)
         found = sbuf[0]
         sbuf[1] = scores(which, row, 1)
         values = cached_values(row)
         soften(which, 0, split(found), values)
         found = sbuf[1]
-        if i == 6:
-            sbuf[0] = scores(0, line(2), 0)
+        if i < 7:
+            sbuf[0] = scores(0, line(4 - step if step == 1 else 2), 0)
         soften(which, 1, split(found), values)
     soften_new(0, 0, nbuf[0])
     soften_new(0, 1, nbuf[1])
@@ -480,7 +494,7 @@
         in_specs=[hbm] * 6 + [vmem] * 2,
         out_specs=vmem,
         scratch_shapes=[pltpu.VMEM(shape, kind) for shape, kind in scratch]
-        + [dma((9,)), dma((3, 16)), dma((LINES, 2, 2)), dma((2 * LINES,)), dma((5,)), dma((SENDS,))],
+        + [dma((9,)), dma((3, 16)), dma((LINES, 2, 2 * CHUNKS)), dma((2 * LINES,)), dma((5,)), dma((SENDS,))],
         compiler_params=pltpu.CompilerParams(
             collective_id=0, has_side_effects=True, vmem_limit_bytes=56 << 20
         ),

time: 62.3 us -> 60 us (0.963)
  Pallas kernels: 60.3 us -> 57.9 us
    pallas_call x1, Pallas kernels: 60.3 us -> 57.9 us  [per_device(): pl.pallas_call(kernel, out_shape=jax.ShapeDtypeStruct((ROWS, COLS), bf16)...]
where the time goes in v3:
time: 60 us; the launch traced here: 59.5 us
  Pallas kernels  57.9 us (96%)
  local copies, waits for them, and re-layouts  1.57 us (3%)
    pallas_call x1, Pallas kernels, per_device(): pl.pallas_call(kernel, out_shape=jax.ShapeDtypeStruct((ROWS, COLS), bf16)...  57.9 us
    unnamed x1, local copies, waits for them, and re-layouts  1.57 us

profile of v3, /device:TPU:32, one launch (start us, length us, event | category | flops | bytes accessed | tf_op | source)
XLA Modules:
  0.0 59.5 jit_solution(2419025916554270771)
XLA Ops:
  0.0 57.9 %shard_map.82 = bf16[128,512]{1,0:T(8,128)(2,1)} custom-call(bf16[128,512]{1,0:T(8,128)(2,1)} %x_hbm.1, bf16[8192,512]{1,0:T(8,128)(2,1)} %wq_hbm.1, bf16[64,8192]{1,0:T(8,128)(2,1)} %bitcast.5, bf16[64,8192]{1,0:T(8,128)(2,1)} %bitcast.6, bf16[64,1152]{1,0:T(8,128)(2,1)} %bitcast.7, bf16[64,1152]{1,0:T(8,128)(2,1)} %bitcast.8, s32[1,128]{1,0:T(1,128)} %bitcast.9, ...), custom_call_target="tpu_custom_call" | custom-call | tf_op jit(solution)/shard_map/pallas_call | solution.py:491
  57.9 1.6 %copy.10 = bf16[128,512]{1,0:T(8,128)(2,1)} copy(bf16[128,512]{1,0:T(8,128)(2,1)} %shard_map.82) | data formatting | bytes 262144

commit v4 on v3

--- a/solution.py
+++ b/solution.py
@@ -76,6 +76,17 @@
             device_id=sib, device_id_type=MESH,
         ).wait_recv()
 
+    settled = []
+
+    def settle(end):
+        for number in range(len(settled), end):
+            ref = pending[number]()
+            pltpu.make_async_remote_copy(
+                src_ref=ref, dst_ref=ref, send_sem=send_sem.at[number], recv_sem=one_sem.at[0],
+                device_id=sib, device_id_type=MESH,
+            ).wait_send()
+            settled.append(number)
+
     def local(i, src, dst):
         copy = pltpu.make_async_copy(src, dst, local_sem.at[i])
         copy.start()
@@ -243,8 +254,10 @@
     remote(places.at[0], places.at[1], one_sem.at[0], far)
     second_wave()
     kv_pair(0)
+    first = len(pending)
     tables()
     ring_step(1)
+    second = len(pending)
     kv_pair(1)
     wk_in.wait()
     wv_in.wait()
@@ -260,18 +273,18 @@
         kv_rest(bit, k)
     other_column(0)
     own_column(1)
+    settle(first)
     ring_step(3)
     kv_own_halves(1)
-    kv_forward(away, 0)
     other_column(1)
     own_column(2)
+    settle(second)
     ring_step(4)
     kv_own_halves(2)
-    kv_forward(away, 1)
-    kv_rest(away, 0)
     other_column(2)
     own_column(3)
     own_column(4)
+    kv_forward(away, 0)
     other_column(3)
     other_column(4)
 
@@ -366,7 +379,9 @@
         @pl.when(i == 0)
         def _():
             new_rows()
+            kv_forward(away, 1)
             kv_forward(away, 2)
+            kv_rest(away, 0)
             kv_rest(away, 1)
             arrived(qs.at[1], one_sem.at[2])
 
@@ -432,6 +447,7 @@
     soften_new(0, 0, nbuf[0])
     soften_new(0, 1, nbuf[1])
 
+    settle(len(pending) - 2)
     arrived(st_in, one_sem.at[3])
     arrived(o_in, one_sem.at[4])
     state = st_in[...]
@@ -445,12 +461,7 @@
         mixed = acc[0, rows, :] * near_part + o_in[rows, :].astype(jnp.float32) * far_part
         out_ref[:, HEAD * j : HEAD * (j + 1)] = (mixed / weight_sum).astype(jnp.bfloat16)
 
-    for number, like in enumerate(pending):
-        ref = like()
-        pltpu.make_async_remote_copy(
-            src_ref=ref, dst_ref=ref, send_sem=send_sem.at[number], recv_sem=one_sem.at[0],
-            device_id=sib, device_id_type=MESH,
-        ).wait_send()
+    settle(len(pending))
 
 
 def per_device(

time: 60 us -> 59.5 us (level)
  Pallas kernels: 57.9 us -> 57.3 us
    pallas_call x1, Pallas kernels: 57.9 us -> 57.3 us  [per_device(): pl.pallas_call(kernel, out_shape=jax.ShapeDtypeStruct((ROWS, COLS), bf16)...]
where the time goes in v4:
time: 59.5 us; the launch traced here: 58.8 us
  Pallas kernels  57.3 us (96%)
  local copies, waits for them, and re-layouts  1.57 us (3%)
    pallas_call x1, Pallas kernels, per_device(): pl.pallas_call(kernel, out_shape=jax.ShapeDtypeStruct((ROWS, COLS), bf16)...  57.3 us
    unnamed x1, local copies, waits for them, and re-layouts  1.57 us

profile of v4, /device:TPU:32, one launch (start us, length us, event | category | flops | bytes accessed | tf_op | source)
XLA Modules:
  0.0 58.8 jit_solution(11054899071881043101)
XLA Ops:
  0.0 57.3 %shard_map.82 = bf16[128,512]{1,0:T(8,128)(2,1)} custom-call(bf16[128,512]{1,0:T(8,128)(2,1)} %x_hbm.1, bf16[8192,512]{1,0:T(8,128)(2,1)} %wq_hbm.1, bf16[64,8192]{1,0:T(8,128)(2,1)} %bitcast.5, bf16[64,8192]{1,0:T(8,128)(2,1)} %bitcast.6, bf16[64,1152]{1,0:T(8,128)(2,1)} %bitcast.7, bf16[64,1152]{1,0:T(8,128)(2,1)} %bitcast.8, s32[1,128]{1,0:T(1,128)} %bitcast.9, ...), custom_call_target="tpu_custom_call" | custom-call | tf_op jit(solution)/shard_map/pallas_call | solution.py:502
  57.3 1.6 %copy.10 = bf16[128,512]{1,0:T(8,128)(2,1)} copy(bf16[128,512]{1,0:T(8,128)(2,1)} %shard_map.82) | data formatting | bytes 262144

commit v5 on v4

--- a/solution.py
+++ b/solution.py
@@ -267,14 +267,14 @@
     ring_step(2)
     kv_pair(2)
     kv_own_halves(0)
+    other_column(0)
+    own_column(1)
+    settle(first)
+    ring_step(3)
     for k in range(CHUNKS):
         kv_forward(bit, k)
     for k in range(CHUNKS):
         kv_rest(bit, k)
-    other_column(0)
-    own_column(1)
-    settle(first)
-    ring_step(3)
     kv_own_halves(1)
     other_column(1)
     own_column(2)

time: 59.5 us -> 59.5 us (level)
  no operation moved by 1% of the time
where the time goes in v5:
time: 59.5 us; the launch traced here: 58.8 us
  Pallas kernels  57.3 us (96%)
  local copies, waits for them, and re-layouts  1.57 us (3%)
    pallas_call x1, Pallas kernels, per_device(): pl.pallas_call(kernel, out_shape=jax.ShapeDtypeStruct((ROWS, COLS), bf16)...  57.3 us
    unnamed x1, local copies, waits for them, and re-layouts  1.57 us

profile of v5, /device:TPU:32, one launch (start us, length us, event | category | flops | bytes accessed | tf_op | source)
XLA Modules:
  0.0 58.8 jit_solution(10291724477782834995)
XLA Ops:
  0.0 57.3 %shard_map.82 = bf16[128,512]{1,0:T(8,128)(2,1)} custom-call(bf16[128,512]{1,0:T(8,128)(2,1)} %x_hbm.1, bf16[8192,512]{1,0:T(8,128)(2,1)} %wq_hbm.1, bf16[64,8192]{1,0:T(8,128)(2,1)} %bitcast.5, bf16[64,8192]{1,0:T(8,128)(2,1)} %bitcast.6, bf16[64,1152]{1,0:T(8,128)(2,1)} %bitcast.7, bf16[64,1152]{1,0:T(8,128)(2,1)} %bitcast.8, s32[1,128]{1,0:T(1,128)} %bitcast.9, ...), custom_call_target="tpu_custom_call" | custom-call | tf_op jit(solution)/shard_map/pallas_call | solution.py:502
  57.3 1.6 %copy.10 = bf16[128,512]{1,0:T(8,128)(2,1)} copy(bf16[128,512]{1,0:T(8,128)(2,1)} %shard_map.82) | data formatting | bytes 262144
